TPU v7x, 256 devices: a whole 4x4x8 slice. The times are simulated.
256 devices in a mesh: plane: 2 (over core), row: 8 (over z), col: 16 (over y, x).
Axes of the slice: x: 4, y: 4, z: 8, core: 2. Of those that a mesh axis runs over, the one named last changes fastest.
Arguments:
- velocity: float32 [3, 4, 4096, 4096], P(None, 'plane', 'row', 'col'), may hold values from -60 to 60
Outputs:
- dissipation: float32 [4, 4096, 4096], P('plane', 'row', 'col')
- fine_means: float32 [128, 128], P('row', 'col')
- coarse_means: float32 [4, 4], replicated
All inputs are finite; a program needn't handle non-finite values.
Results may differ from a plain program's by a relative error of at most 0.000078.
Values sent between devices are 32-bit elements; how exact they have to be, the bound alone decides.
No kernel may reach another device: no remote copies, remote signals or barrier semaphores. Data moves between devices by JAX's collectives and lax.ppermute only.
A program may use at most 128 MiB of HBM per device.

v0:
```python
import functools
import math
import jax
import jax.numpy as jnp
from jax import lax
from jax.sharding import Mesh
from jax.sharding import PartitionSpec as P

N = 4096
FIRST = 32
FINE = 32
COARSE = 1024
PLANE_COL = ("plane", "col_0", "col_1")
COL = ("col_0", "col_1")
ROW_COL = ("row", "col_0", "col_1")
precise = lax.Precision.HIGHEST


def split_up(shard, dim, size):
    lengths = shard.shape
    blocks = shard.reshape(*lengths[:dim], size, lengths[dim] // size, *lengths[dim + 1 :])
    return jnp.moveaxis(blocks, dim, 0)


def cut_rows(length, count):
    turn = length // count
    if turn >= 8:
        turn -= turn % 8
    return [turn * k for k in range(1, count)]


def in_order(blocks, dim):
    lengths = list(blocks.shape[1:])
    lengths[dim] *= blocks.shape[0]
    return jnp.moveaxis(blocks, 0, dim).reshape(lengths)


def exchange_in_pieces(shard, axis, pieces, split_dim, concat_dim):
    blocks = split_up(shard, split_dim, lax.axis_size(axis))
    widest = max(range(1, max(2, blocks.ndim - 1)), key=lambda d: blocks.shape[d])
    outs = []
    for share in jnp.split(blocks, cut_rows(blocks.shape[widest], pieces), axis=widest):
        if share.size:
            outs.append(lax.all_to_all(share, axis, split_axis=0, concat_axis=0, tiled=True))
    return in_order(jnp.concatenate(outs, axis=widest), concat_dim)


def exchange_both(shard, axis, axes, splits, concats):
    sizes = [lax.axis_size(a) for a in axes]
    blocks = split_up(shard, splits[0], sizes[0])
    blocks = jnp.moveaxis(split_up(blocks, splits[1] + 1, sizes[1]), 0, 1)
    inside = blocks.shape[2:]
    blocks = blocks.reshape(-1, *inside)
    blocks = lax.all_to_all(blocks, axis, split_axis=0, concat_axis=0, tiled=True)
    blocks = in_order(blocks.reshape(*sizes, *inside), concats[0] + 1)
    return in_order(blocks, concats[1])


def gathered_total(shard, axis):
    return lax.all_gather(shard, axis).sum(0)


def over_axes(shard, axes):
    return functools.reduce(lax.psum, axes, shard)


def angle_table(height, across, modulus):
    left_idx = lax.broadcasted_iota(jnp.int32, (height, across), 0)
    right_idx = lax.broadcasted_iota(jnp.int32, (height, across), 1)
    turn_count = left_idx * right_idx % modulus
    phase_ang = turn_count.astype(jnp.float32) * (2.0 * math.pi / modulus)
    return (jnp.cos(phase_ang), jnp.sin(phase_ang))


def wave_table(first_len, second, length):
    low_idx = lax.broadcasted_iota(jnp.int32, (first_len, second), 0)
    high_idx = lax.broadcasted_iota(jnp.int32, (first_len, second), 1)
    indices = low_idx + first_len * high_idx
    signed = jnp.where(indices < length // 2, indices, indices - length)
    signed = jnp.where(indices == length // 2, 0, signed)
    return signed.astype(jnp.float32) * (2.0 * math.pi / length)


def left_mult(coeffs, values):
    return jnp.einsum("kn,...nm->...km", coeffs, values, precision=precise)


def right_mult(values, coeffs):
    return jnp.einsum("...kn,nm->...km", values, coeffs, precision=precise)


def derivative_last(values):
    length = values.shape[-1]
    first_len = FIRST
    second = length // first_len
    leading = values.shape[:-1]
    blocks = values.reshape(leading + (first_len, second))
    cos_a, sin_a = angle_table(first_len, first_len, first_len)
    cos_b, sin_b = angle_table(second, second, second)
    cos_t, sin_t = angle_table(first_len, second, length)
    forward_a = jnp.concatenate([cos_a, -sin_a], axis=0)
    section_a = left_mult(forward_a, blocks)
    real_a = section_a[..., :first_len, :]
    imag_a = section_a[..., first_len:, :]
    real_b = real_a * cos_t + imag_a * sin_t
    imag_b = imag_a * cos_t - real_a * sin_t
    forward_b = jnp.concatenate(
        [jnp.concatenate([cos_b, -sin_b], axis=1), jnp.concatenate([sin_b, cos_b], axis=1)], axis=0
    )
    section_c = right_mult(jnp.concatenate([real_b, imag_b], axis=-1), forward_b)
    wavenum = wave_table(first_len, second, length)
    scaled = jnp.concatenate(
        [-wavenum * section_c[..., second:], wavenum * section_c[..., :second]], axis=-1
    )
    inverse_b = jnp.concatenate(
        [jnp.concatenate([cos_b, sin_b], axis=1), jnp.concatenate([-sin_b, cos_b], axis=1)], axis=0
    )
    section_e = right_mult(scaled, inverse_b)
    real_e = section_e[..., :second]
    imag_e = section_e[..., second:]
    real_f = real_e * cos_t - imag_e * sin_t
    imag_f = real_e * sin_t + imag_e * cos_t
    inverse_a = jnp.concatenate([cos_a, -sin_a], axis=1)
    result = left_mult(inverse_a, jnp.concatenate([real_f, imag_f], axis=-2)) * (1.0 / length)
    return result.reshape(leading + (length,))


def along_rows(pencil):
    turned = jnp.swapaxes(pencil, 2, 3)
    back_turned = jnp.swapaxes(derivative_last(turned), 2, 3)
    return exchange_in_pieces(back_turned, "row", 2, 2, 3)


def per_device(velocity):
    x_local = velocity.shape[2]
    y_local = velocity.shape[3]
    plane_count = velocity.shape[1] * lax.axis_size("plane")
    grad_x = along_rows(lax.all_to_all(velocity, "row", split_axis=3, concat_axis=2, tiled=True))
    slab_data = exchange_both(velocity, PLANE_COL, ("plane", COL), (2, 2), (1, 3))
    slab_y = derivative_last(slab_data)
    slab_z = (jnp.roll(slab_data, -1, axis=1) - jnp.roll(slab_data, 1, axis=1)) * 0.5
    cross_yz = slab_z[1] + slab_y[2]
    partial_value = slab_y[1] * slab_y[1] + slab_z[2] * slab_z[2] + 0.5 * cross_yz * cross_yz
    packed = jnp.stack([partial_value, slab_y[0], slab_z[0]])
    packed = lax.all_to_all(packed, COL, split_axis=3, concat_axis=2, tiled=True)
    packed = lax.all_to_all(packed, "plane", split_axis=1, concat_axis=2, tiled=True)
    cross_xy = packed[1] + grad_x[1]
    cross_xz = packed[2] + grad_x[2]
    dissip = packed[0] + grad_x[0] * grad_x[0]
    dissip = dissip + 0.5 * (cross_xy * cross_xy + cross_xz * cross_xz)
    column_sum = jnp.sum(dissip, axis=0)
    fine_local = column_sum.reshape(x_local // FINE, FINE, y_local // FINE, FINE).sum(axis=(1, 3))
    fine_total = gathered_total(fine_local, "plane")
    fine_means = fine_total * (1.0 / (plane_count * FINE * FINE))
    local_total = jnp.sum(fine_total)
    box_count = N // COARSE
    box_row = lax.axis_index("row") * x_local // COARSE
    box_col = lax.axis_index(COL) * y_local // COARSE
    rows_hit = (lax.iota(jnp.int32, box_count) == box_row).astype(jnp.float32)
    cols_hit = (lax.iota(jnp.int32, box_count) == box_col).astype(jnp.float32)
    partial_map = rows_hit[:, None] * cols_hit[None, :] * local_total
    coarse_total = over_axes(partial_map, ROW_COL)
    coarse_means = coarse_total * (1.0 / (plane_count * COARSE * COARSE))
    return (dissip, fine_means, coarse_means)


def solution(mesh):
    split = Mesh(
        mesh.devices.reshape(mesh.shape["plane"], mesh.shape["row"], 4, 4),
        ("plane", "row", "col_0", "col_1"),
    )
    in_specs = (P(None, "plane", "row", COL),)
    out_specs = (P("plane", "row", COL), P("row", COL), P())
    return jax.shard_map(
        per_device, mesh=split, in_specs=in_specs, out_specs=out_specs, check_vma=False
    )
```

profile of v0, /device:TPU:2, one launch (start us, length us, event | category | flops | bytes accessed | tf_op | source)
XLA Modules:
  0.0 436.9 jit_solution(4735583663950403906)
XLA Ops:
  4.6 7.9 %all-to-all-start = ((f32[32,3,2,16,256]{4,3,2,1,0:T(8,128)}), f32[32,3,2,16,256]{4,3,2,1,0:T(8,128)}, u32[]{:S(2)}, u32[]{:S(2)}) async-start(f32[32,3,2,16,256]{4,3,2,1,0:T(8,128)} %bitcast.121), calls=%async_computation | async-start | bytes 6291456 | tf_op jit(solution)/shard_map/all_to_all | solution.py:54
  16.9 34.7 %all-to-all-done = f32[32,3,2,16,256]{4,3,2,1,0:T(8,128)} async-done(((f32[32,3,2,16,256]{4,3,2,1,0:T(8,128)}), f32[32,3,2,16,256]{4,3,2,1,0:T(8,128)}, u32[]{:S(2)}, u32[]{:S(2)}) %all-to-all-start) | async-done | bytes 3145760 | tf_op jit(solution)/shard_map/all_to_all | solution.py:54
  51.6 8.5 %all-to-all-start.3 = ((f32[3,2,512,256]{2,1,0,3:T(2,128)}), f32[3,2,512,256]{2,1,0,3:T(2,128)}, u32[]{:S(2)}, u32[]{:S(2)}) async-start(f32[3,2,512,256]{2,1,0,3:T(2,128)} %copy.102), calls=%async_computation.3 | async-start | bytes 6291456 | tf_op jit(solution)/shard_map/all_to_all | solution.py:138
  66.1 4.9 %reshape_reshape.3 = f32[3,4,16,32,128]{4,3,2,1,0:T(8,128)} reshape(f32[3,4,16,16,256]{4,3,2,1,0:T(8,128)} %copy.93) | data formatting | bytes 6291456 | tf_op jit(solution)/shard_map/reshape;reshape | solution.py:97
  71.0 7.3 %convolution_bitcast_fusion.1 = f32[3,4,16,64,128]{4,3,2,1,0:T(8,128)S(1)} fusion(f32[3,4,16,32,128]{4,3,2,1,0:T(8,128)} %reshape_reshape.3, f32[32,32]{0,1:T(8,128)S(1)} %get-tuple-element.40, f32[32,32]{0,1:T(8,128)S(1)} %get-tuple-element.41), kind=kOutput, calls=%fused_computation.44 | convolution fusion | flops 603981824 | bytes 9445376 | tf_op jit(solution)/shard_map/kn,...nm->...km/dot_general | solution.py:85
  79.5 5.3 %fusion = f32[3,4,16,32,256]{4,3,2,1,0:T(8,128)S(1)} fusion(f32[3,4,16,32,128]{4,3,2,1,0:T(8,128)S(1)} %get-tuple-element.15, f32[3,4,16,32,128]{4,3,2,1,0:T(8,128)S(1)} %get-tuple-element.14, f32[128,128]{1,0:T(8,128)S(1)} %get-tuple-element.45, f32[128,128]{1,0:T(8,128)S(1)} %get-tuple-element.44, f32[128,128]{1,0:T(8,128)S(1)} %fusion.47), kind=kOutput, calls=%fused_computation | convolution fusion | flops 4833607680 | bytes 12779520 | tf_op jit(solution)/shard_map/...kn,nm->...km/dot_general | solution.py:89
  85.7 5.5 %fusion.4 = f32[3,4,16,32,256]{4,3,2,1,0:T(8,128)S(1)} fusion(f32[3,4,16,32,128]{4,3,2,1,0:T(8,128)S(1)} %get-tuple-element.19, f32[3,4,16,32,128]{4,3,2,1,0:T(8,128)S(1)} %get-tuple-element.18, f32[128,128]{1,0:T(8,128)S(1)} %get-tuple-element.45, f32[128,128]{1,0:T(8,128)S(1)} %fusion.47, f32[128,128]{1,0:T(8,128)S(1)} %get-tuple-element.44), kind=kOutput, calls=%fused_computation.4 | convolution fusion | flops 4833607680 | bytes 12779520 | tf_op jit(solution)/shard_map/...kn,nm->...km/dot_general | solution.py:89
  112.4 16.9 %copy.96 = f32[3,4,16,4096]{2,1,0,3:T(4,128)} copy(f32[3,4,16,4096]{3,2,1,0:T(8,128)S(1)} %pad_maximum_fusion) | data formatting | bytes 6291456 | tf_op jit(solution)/shard_map/stack | solution.py:144
  129.2 23.6 %reshape.184 = f32[16,1,49152]{2,1,0:T(1,128)} reshape(f32[4096,3,4,16]{3,2,1,0:T(4,128)} %bitcast.112) | data formatting | bytes 6291456
  152.8 6.8 %all-to-all-start.1 = ((f32[16,1,49152]{2,1,0:T(1,128)}), f32[16,1,49152]{2,1,0:T(1,128)S(1)}, u32[]{:S(2)}, u32[]{:S(2)}) async-start(f32[16,1,49152]{2,1,0:T(1,128)} %reshape.184), calls=%async_computation.1 | async-start | bytes 6291456 | tf_op jit(solution)/shard_map/all_to_all | solution.py:145
  163.1 5.4 %convolution_bitcast_fusion = f32[3,2,32,64,128]{4,3,2,1,0:T(8,128)S(1)} fusion(f32[3,2,32,32,128]{4,3,2,1,0:T(8,128)S(1)} %bitcast.126, f32[32,32]{0,1:T(8,128)S(1)} %get-tuple-element.40, f32[32,32]{0,1:T(8,128)S(1)} %get-tuple-element.41), kind=kOutput, calls=%fused_computation.43 | convolution fusion | flops 603981824 | bytes 9445376 | tf_op jit(solution)/shard_map/kn,...nm->...km/dot_general | solution.py:85
  169.7 5.5 %fusion.12 = f32[3,2,32,32,256]{4,3,2,1,0:T(8,128)S(1)} fusion(f32[3,2,32,32,128]{4,3,2,1,0:T(8,128)S(1)} %get-tuple-element.11, f32[3,2,32,32,128]{4,3,2,1,0:T(8,128)S(1)} %get-tuple-element.10, f32[128,128]{1,0:T(8,128)S(1)} %get-tuple-element.45, f32[128,128]{1,0:T(8,128)S(1)} %get-tuple-element.44, f32[128,128]{1,0:T(8,128)S(1)} %fusion.47), kind=kOutput, calls=%fused_computation.12 | convolution fusion | flops 4833607680 | bytes 12779520 | tf_op jit(solution)/shard_map/...kn,nm->...km/dot_general | solution.py:89
  176.1 5.3 %fusion.16 = f32[3,2,32,32,256]{4,3,2,1,0:T(8,128)S(1)} fusion(f32[3,2,32,32,128]{4,3,2,1,0:T(8,128)S(1)} %get-tuple-element.17, f32[3,2,32,32,128]{4,3,2,1,0:T(8,128)S(1)} %get-tuple-element.16, f32[128,128]{1,0:T(8,128)S(1)} %get-tuple-element.45, f32[128,128]{1,0:T(8,128)S(1)} %fusion.47, f32[128,128]{1,0:T(8,128)S(1)} %get-tuple-element.44), kind=kOutput, calls=%fused_computation.16 | convolution fusion | flops 4833607680 | bytes 12779520 | tf_op jit(solution)/shard_map/...kn,nm->...km/dot_general | solution.py:89
  182.4 5.2 %multiply_bitcast_fusion = f32[3,2,32,32,128]{4,3,2,1,0:T(8,128)} fusion(f32[3,2,32,32,128]{4,3,2,1,0:T(8,128)S(1)} %get-tuple-element.9, f32[3,2,32,32,128]{4,3,2,1,0:T(8,128)S(1)} %get-tuple-element.8, f32[32,32]{0,1:T(8,128)S(1)} %get-tuple-element.40, f32[32,32]{0,1:T(8,128)S(1)} %get-tuple-element.41), kind=kOutput, calls=%fused_computation.33 | convolution fusion | flops 606341120 | bytes 9445376 | tf_op jit(solution)/shard_map/kn,...nm->...km/dot_general | solution.py:85
  204.9 10.1 %reduce.5 = f32[16,49152]{1,0:T(8,128)S(1)} reduce(f32[16,1,49152]{2,1,0:T(1,128)} %copy-done.2, f32[]{:T(128)} %broadcast.212), dimensions={1}, to_apply=%all_to_all.47.reduce_sub_computation | reduce | bytes 6291460 | tf_op jit(solution)/shard_map/all_to_all | solution.py:145
  215.0 27.0 %reshape.185 = f32[4096,3,4,16]{3,2,1,0:T(4,128)} reshape(f32[16,49152]{1,0:T(8,128)S(1)} %reduce.5) | data formatting | bytes 6291456
  242.0 19.5 %copy.128 = f32[3,4,16,16,256]{4,2,3,0,1:T(8,128)S(1)} copy(f32[3,4,16,16,256]{2,1,0,4,3:T(4,128)} %bitcast.113) | data formatting | bytes 6291456 | tf_op jit(solution)/shard_map/all_to_all | solution.py:145
  261.5 7.2 %all_to_all.66 = f32[3,4,256,256]{3,2,0,1:T(8,128)} all-to-all(f32[3,4,256,256]{3,2,0,1:T(8,128)S(1)} %bitcast.119), channel_id=1, replica_groups=mesh['plane'=2,'row'=8,'col_0'=4,'col_1'=4] {'plane'}, dimensions={1} | all-to-all | bytes 6291456 | tf_op jit(solution)/shard_map/all_to_all | solution.py:146
  268.8 6.2 %all-to-all-start.4 = ((f32[8,3,2,256,32]{3,4,2,1,0:T(8,128)}), f32[8,3,2,256,32]{3,4,2,1,0:T(8,128)S(1)}, u32[]{:S(2)}, u32[]{:S(2)}) async-start(f32[8,3,2,256,32]{3,4,2,1,0:T(8,128)} %copy.106), calls=%async_computation.4 | async-start | bytes 3145728 | tf_op jit(solution)/shard_map/all_to_all | solution.py:44
  276.6 38.6 %all-to-all-done.4 = f32[8,3,2,256,32]{3,4,2,1,0:T(8,128)S(1)} async-done(((f32[8,3,2,256,32]{3,4,2,1,0:T(8,128)}), f32[8,3,2,256,32]{3,4,2,1,0:T(8,128)S(1)}, u32[]{:S(2)}, u32[]{:S(2)}) %all-to-all-start.4) | async-done | bytes 1572896 | tf_op jit(solution)/shard_map/all_to_all | solution.py:44
  322.0 38.1 %all-to-all-done.5 = f32[8,3,2,256,32]{3,4,2,1,0:T(8,128)} async-done(((f32[8,3,2,256,32]{3,4,2,1,0:T(8,128)}), f32[8,3,2,256,32]{3,4,2,1,0:T(8,128)}, u32[]{:S(2)}, u32[]{:S(2)}) %all-to-all-start.5) | async-done | bytes 1572896 | tf_op jit(solution)/shard_map/all_to_all | solution.py:44
  394.9 14.7 %psum.21 = f32[4,4]{1,0:T(4,128)S(1)} all-reduce(f32[4,4]{1,0:T(4,128)S(1)} %multiply_multiply_fusion.1), channel_id=1, replica_groups=mesh['plane'=2,'row'=8,'col_0'=4,'col_1'=4] {'row'}, use_global_device_ids=true, to_apply=%region_4.5 | all-reduce | flops 16 | bytes 128 | tf_op jit(solution)/shard_map/psum | solution.py:64
  409.6 9.3 %psum.22 = f32[4,4]{1,0:T(4,128)S(1)} all-reduce(f32[4,4]{1,0:T(4,128)S(1)} %psum.21), channel_id=1, replica_groups=mesh['plane'=2,'row'=8,'col_0'=4,'col_1'=4] {'col_0'}, use_global_device_ids=true, to_apply=%region_5.6 | all-reduce | flops 16 | bytes 128 | tf_op jit(solution)/shard_map/psum | solution.py:64
  418.9 12.8 %psum.23 = f32[4,4]{1,0:T(4,128)S(1)} all-reduce(f32[4,4]{1,0:T(4,128)S(1)} %psum.22), channel_id=1, replica_groups=mesh['plane'=2,'row'=8,'col_0'=4,'col_1'=4] {'col_1'}, use_global_device_ids=true, to_apply=%region_6.7 | all-reduce | flops 16 | bytes 128 | tf_op jit(solution)/shard_map/psum | solution.py:64
  (89 shorter events, 109.4 us)
Async XLA Ops:
  4.6 7.9 %copy-start.1 = (f32[3,2,512,256]{3,2,1,0:T(8,128)S(1)}, f32[3,2,512,256]{3,2,1,0:T(8,128)}, u32[]{:S(2)}) copy-start(f32[3,2,512,256]{3,2,1,0:T(8,128)} %param.1) | copy-start | bytes 9437188
  4.6 46.9 %all-to-all-start = ((f32[32,3,2,16,256]{4,3,2,1,0:T(8,128)}), f32[32,3,2,16,256]{4,3,2,1,0:T(8,128)}, u32[]{:S(2)}, u32[]{:S(2)}) async-start(f32[32,3,2,16,256]{4,3,2,1,0:T(8,128)} %bitcast.121), calls=%async_computation | async-start | bytes 6291456 | tf_op jit(solution)/shard_map/all_to_all | solution.py:54
  51.6 101.3 %all-to-all-start.3 = ((f32[3,2,512,256]{2,1,0,3:T(2,128)}), f32[3,2,512,256]{2,1,0,3:T(2,128)}, u32[]{:S(2)}, u32[]{:S(2)}) async-start(f32[3,2,512,256]{2,1,0,3:T(2,128)} %copy.102), calls=%async_computation.3 | async-start | bytes 6291456 | tf_op jit(solution)/shard_map/all_to_all | solution.py:138
  104.7 4.1 copy-start
  109.3 1.2 copy-start.9
  109.3 1.5 copy-start.10
  110.9 1.2 copy-start.11
  152.8 49.9 %all-to-all-start.1 = ((f32[16,1,49152]{2,1,0:T(1,128)}), f32[16,1,49152]{2,1,0:T(1,128)S(1)}, u32[]{:S(2)}, u32[]{:S(2)}) async-start(f32[16,1,49152]{2,1,0:T(1,128)} %reshape.184), calls=%async_computation.1 | async-start | bytes 6291456 | tf_op jit(solution)/shard_map/all_to_all | solution.py:145
  202.8 1.7 copy-start.2
  268.8 6.2 %copy-start.7 = (f32[8,3,2,256,32]{3,0,4,2,1:T(8,128)S(1)}, f32[8,3,2,256,32]{3,0,4,2,1:T(8,128)}, u32[]{:S(2)}) copy-start(f32[8,3,2,256,32]{3,0,4,2,1:T(8,128)} %get-tuple-element.28) | copy-start | bytes 4718596
  268.8 46.5 %all-to-all-start.4 = ((f32[8,3,2,256,32]{3,4,2,1,0:T(8,128)}), f32[8,3,2,256,32]{3,4,2,1,0:T(8,128)S(1)}, u32[]{:S(2)}, u32[]{:S(2)}) async-start(f32[8,3,2,256,32]{3,4,2,1,0:T(8,128)} %copy.106), calls=%async_computation.4 | async-start | bytes 3145728 | tf_op jit(solution)/shard_map/all_to_all | solution.py:44
  315.2 4.5 %copy-start.6 = (f32[8,3,2,256,32]{3,4,2,1,0:T(8,128)}, f32[8,3,2,256,32]{3,4,2,1,0:T(8,128)S(1)}, u32[]{:S(2)}) copy-start(f32[8,3,2,256,32]{3,4,2,1,0:T(8,128)S(1)} %all-to-all-done.4) | copy-start | bytes 4718596
  315.2 44.9 %all-to-all-start.5 = ((f32[8,3,2,256,32]{3,4,2,1,0:T(8,128)}), f32[8,3,2,256,32]{3,4,2,1,0:T(8,128)}, u32[]{:S(2)}, u32[]{:S(2)}) async-start(f32[8,3,2,256,32]{3,4,2,1,0:T(8,128)} %copy.107), calls=%async_computation.5 | async-start | bytes 3145728 | tf_op jit(solution)/shard_map/all_to_all | solution.py:44
  382.7 3.2 copy-start.5
  383.8 3.5 copy-start.4
  384.9 3.7 copy-start.3
  388.6 44.3 %copy-start.8 = (f32[1,2,2,256,256]{4,3,2,1,0:T(8,128)S(1)}, f32[1,2,2,256,256]{4,3,2,1,0:T(8,128)}, u32[]{:S(2)}) copy-start(f32[1,2,2,256,256]{4,3,2,1,0:T(8,128)} %copy.101) | copy-start | bytes 3145732
where the time goes:
time: 443 us; the launch traced here: 437 us
  local copies, waits for them, and re-layouts  165 us (37%)
  waiting for transfers between devices  114 us (26%)
  blocking collectives  45.8 us (10%)
  matrix products  43.5 us (10%)
  starting transfers between devices  33.8 us (8%)
  other arithmetic  33.5 us (8%)
    all_to_all x2, waiting for transfers between devices, exchange_in_pieces(): lax.all_to_all(share, axis, split_axis=0, concat_axis=0, tiled=True)  76.7 us
    unnamed x29, local copies, waits for them, and re-layouts  62.9 us
    psum x3, blocking collectives, over_axes(): return functools.reduce(lax.psum, axes, shard)  36.8 us
    all_to_all x1, waiting for transfers between devices, exchange_both(): lax.all_to_all(blocks, axis, split_axis=0, concat_axis=0, tiled=True)  34.7 us
    dot_general x4, matrix products, left_mult(): return jnp.einsum('kn,...nm->...km', coeffs, values, precision=precise)  21.7 us
    dot_general x4, matrix products, right_mult(): return jnp.einsum('...kn,nm->...km', values, coeffs, precision=precise)  21.7 us
    all_to_all x2, local copies, waits for them, and re-layouts, per_device(): lax.all_to_all(packed, COL, split_axis=3, concat_axis=2, tiled=True)  20 us
    another operation x1, local copies, waits for them, and re-layouts, per_device(): packed = jnp.stack([partial_value, slab_y[0], slab_z[0]])  16.9 us
  transfers between devices with their start and end apart: 5, of which 4 were waited for; matrix products, arithmetic and copies ran while one was open for 32% of the time, Pallas kernels for 0%

commit v1 on v0

--- a/solution.py
+++ b/solution.py
@@ -142,7 +142,9 @@
     cross_yz = slab_z[1] + slab_y[2]
     partial_value = slab_y[1] * slab_y[1] + slab_z[2] * slab_z[2] + 0.5 * cross_yz * cross_yz
     packed = jnp.stack([partial_value, slab_y[0], slab_z[0]])
-    packed = lax.all_to_all(packed, COL, split_axis=3, concat_axis=2, tiled=True)
+    packed = jnp.concatenate(
+        lax.all_to_all(jnp.stack(jnp.split(packed, lax.axis_size(COL), axis=3)), COL, 0, 0), axis=2
+    )
     packed = lax.all_to_all(packed, "plane", split_axis=1, concat_axis=2, tiled=True)
     cross_xy = packed[1] + grad_x[1]
     cross_xz = packed[2] + grad_x[2]

time: 443 us -> 364 us (0.82)
  local copies, waits for them, and re-layouts: 165 us -> 81.2 us
  waiting for transfers between devices: 114 us -> 128 us
  other arithmetic: 33.5 us -> 27.6 us
    unnamed x29 -> x40, local copies, waits for them, and re-layouts: 62.9 us -> 17.2 us
    all_to_all x2 -> x0, local copies, waits for them, and re-layouts: 20 us -> none  [per_device(): lax.all_to_all(packed, COL, split_axis=3, concat_axis=2, tiled=True)]
    another operation x1, local copies, waits for them, and re-layouts: 16.9 us -> 0.68 us  [per_device(): jnp.stack(jnp.split(packed, lax.axis_size(COL), axis=3))]
    all_to_all x1 -> x0, other arithmetic: 10.1 us -> none  [per_device(): lax.all_to_all(packed, COL, split_axis=3, concat_axis=2, tiled=True)]
    all_to_all x1, waiting for transfers between devices: 2.54 us -> 10.4 us  [per_device(): lax.all_to_all(jnp.stack(jnp.split(packed, lax.axis_size(COL), axis=3)),...]
    all_to_all x1, waiting for transfers between devices: 0.01 us -> 7.83 us  [per_device(): lax.all_to_all(velocity, 'row', split_axis=3, concat_axis=2, tiled=True)]
  transfers between devices with their start and end apart: 5 -> 5, of which waited for: 4 -> 5; matrix products, arithmetic and copies ran while one was open for 32% -> 30% of each run, Pallas kernels for 0% -> 0%
where the time goes in v1:
time: 364 us; the launch traced here: 358 us
  waiting for transfers between devices  128 us (35%)
  local copies, waits for them, and re-layouts  81.2 us (22%)
  blocking collectives  45.5 us (12%)
  matrix products  43.7 us (12%)
  starting transfers between devices  31.4 us (9%)
  other arithmetic  27.6 us (8%)
    all_to_all x2, waiting for transfers between devices, exchange_in_pieces(): lax.all_to_all(share, axis, split_axis=0, concat_axis=0, tiled=True)  74.7 us
    psum x3, blocking collectives, over_axes(): return functools.reduce(lax.psum, axes, shard)  36.4 us
    all_to_all x1, waiting for transfers between devices, exchange_both(): lax.all_to_all(blocks, axis, split_axis=0, concat_axis=0, tiled=True)  34.7 us
    dot_general x4, matrix products, right_mult(): return jnp.einsum('...kn,nm->...km', values, coeffs, precision=precise)  22 us
    dot_general x4, matrix products, left_mult(): return jnp.einsum('kn,...nm->...km', coeffs, values, precision=precise)  21.7 us
    unnamed x40, local copies, waits for them, and re-layouts  17.2 us
    all_to_all x1, waiting for transfers between devices, per_device(): lax.all_to_all(jnp.stack(jnp.split(packed, lax.axis_size(COL), axis=3)),...  10.4 us
    all_to_all x1, starting transfers between devices, per_device(): lax.all_to_all(velocity, 'row', split_axis=3, concat_axis=2, tiled=True)  8.47 us
  transfers between devices with their start and end apart: 5, of which 5 were waited for; matrix products, arithmetic and copies ran while one was open for 30% of the time, Pallas kernels for 0%

profile of v1, /device:TPU:2, one launch (start us, length us, event | category | flops | bytes accessed | tf_op | source)
XLA Modules:
  0.0 358.4 jit_solution(1505324255066678966)
XLA Ops:
  0.6 4.0 %copy.118 = f32[2,16,3,2,16,256]{5,4,3,2,1,0:T(8,128)} copy(f32[2,16,3,2,16,256]{5,4,1,0,3,2:T(8,128)} %bitcast.176) | data formatting | bytes 6291456 | tf_op jit(solution)/shard_map/transpose;transpose | solution.py:51
  4.7 7.9 %all-to-all-start = ((f32[32,3,2,16,256]{4,3,2,1,0:T(8,128)}), f32[32,3,2,16,256]{4,3,2,1,0:T(8,128)}, u32[]{:S(2)}, u32[]{:S(2)}) async-start(f32[32,3,2,16,256]{4,3,2,1,0:T(8,128)} %bitcast.177), calls=%async_computation | async-start | bytes 6291456 | tf_op jit(solution)/shard_map/all_to_all | solution.py:54
  16.9 34.7 %all-to-all-done = f32[32,3,2,16,256]{4,3,2,1,0:T(8,128)} async-done(((f32[32,3,2,16,256]{4,3,2,1,0:T(8,128)}), f32[32,3,2,16,256]{4,3,2,1,0:T(8,128)}, u32[]{:S(2)}, u32[]{:S(2)}) %all-to-all-start) | async-done | bytes 3145760 | tf_op jit(solution)/shard_map/all_to_all | solution.py:54
  51.6 8.5 %all-to-all-start.3 = ((f32[3,2,512,256]{2,1,0,3:T(2,128)}), f32[3,2,512,256]{2,1,0,3:T(2,128)S(1)}, u32[]{:S(2)}, u32[]{:S(2)}) async-start(f32[3,2,512,256]{2,1,0,3:T(2,128)} %copy.127), calls=%async_computation.3 | async-start | bytes 6291456 | tf_op jit(solution)/shard_map/all_to_all | solution.py:138
  67.0 3.9 %copy.120 = f32[3,4,16,16,256]{4,3,2,1,0:T(8,128)} copy(f32[3,4,16,16,256]{4,2,1,0,3:T(8,128)S(1)} %bitcast.172) | data formatting | bytes 6291456 | tf_op jit(solution)/shard_map/transpose | solution.py:35
  70.9 4.7 %reshape_reshape.3 = f32[3,4,16,32,128]{4,3,2,1,0:T(8,128)} reshape(f32[3,4,16,16,256]{4,3,2,1,0:T(8,128)} %copy.120) | data formatting | bytes 6291456 | tf_op jit(solution)/shard_map/reshape;reshape | solution.py:97
  75.5 7.3 %convolution_bitcast_fusion.1 = f32[3,4,16,64,128]{4,3,2,1,0:T(8,128)S(1)} fusion(f32[3,4,16,32,128]{4,3,2,1,0:T(8,128)} %reshape_reshape.3, f32[32,32]{0,1:T(8,128)S(1)} %get-tuple-element.40, f32[32,32]{0,1:T(8,128)S(1)} %get-tuple-element.41), kind=kOutput, calls=%fused_computation.44 | convolution fusion | flops 603981824 | bytes 9445376 | tf_op jit(solution)/shard_map/kn,...nm->...km/dot_general | solution.py:85
  84.0 5.3 %fusion = f32[3,4,16,32,256]{4,3,2,1,0:T(8,128)S(1)} fusion(f32[3,4,16,32,128]{4,3,2,1,0:T(8,128)S(1)} %get-tuple-element.15, f32[3,4,16,32,128]{4,3,2,1,0:T(8,128)S(1)} %get-tuple-element.14, f32[128,128]{1,0:T(8,128)S(1)} %get-tuple-element.45, f32[128,128]{1,0:T(8,128)S(1)} %get-tuple-element.44, f32[128,128]{1,0:T(8,128)S(1)} %fusion.63), kind=kOutput, calls=%fused_computation | convolution fusion | flops 4833607680 | bytes 12779520 | tf_op jit(solution)/shard_map/...kn,nm->...km/dot_general | solution.py:89
  90.3 5.8 %fusion.4 = f32[3,4,16,32,256]{4,3,2,1,0:T(8,128)S(1)} fusion(f32[3,4,16,32,128]{4,3,2,1,0:T(8,128)S(1)} %get-tuple-element.19, f32[3,4,16,32,128]{4,3,2,1,0:T(8,128)S(1)} %get-tuple-element.18, f32[128,128]{1,0:T(8,128)S(1)} %get-tuple-element.45, f32[128,128]{1,0:T(8,128)S(1)} %fusion.63, f32[128,128]{1,0:T(8,128)S(1)} %get-tuple-element.44), kind=kOutput, calls=%fused_computation.4 | convolution fusion | flops 4833607680 | bytes 12779520 | tf_op jit(solution)/shard_map/...kn,nm->...km/dot_general | solution.py:89
  126.2 7.8 %all-to-all-done.3 = f32[3,2,512,256]{2,1,0,3:T(2,128)S(1)} async-done(((f32[3,2,512,256]{2,1,0,3:T(2,128)}), f32[3,2,512,256]{2,1,0,3:T(2,128)S(1)}, u32[]{:S(2)}, u32[]{:S(2)}) %all-to-all-start.3) | async-done | bytes 3145760 | tf_op jit(solution)/shard_map/all_to_all | solution.py:138
  134.1 7.1 %all-to-all-start.1 = ((f32[16,3,4,16,256]{4,3,2,1,0:T(8,128)}), f32[16,3,4,16,256]{4,3,2,1,0:T(8,128)}, u32[]{:S(2)}, u32[]{:S(2)}) async-start(f32[16,3,4,16,256]{4,3,2,1,0:T(8,128)} %fusion.39), calls=%async_computation.1 | async-start | bytes 6291456 | tf_op jit(solution)/shard_map/all_to_all | solution.py:146
  142.7 5.4 %convolution_bitcast_fusion = f32[3,2,32,64,128]{4,3,2,1,0:T(8,128)S(1)} fusion(f32[3,2,32,32,128]{4,3,2,1,0:T(8,128)S(1)} %bitcast.183, f32[32,32]{0,1:T(8,128)S(1)} %get-tuple-element.40, f32[32,32]{0,1:T(8,128)S(1)} %get-tuple-element.41), kind=kOutput, calls=%fused_computation.43 | convolution fusion | flops 603981824 | bytes 9445376 | tf_op jit(solution)/shard_map/kn,...nm->...km/dot_general | solution.py:85
  149.3 5.6 %fusion.12 = f32[3,2,32,32,256]{4,3,2,1,0:T(8,128)S(1)} fusion(f32[3,2,32,32,128]{4,3,2,1,0:T(8,128)S(1)} %get-tuple-element.11, f32[3,2,32,32,128]{4,3,2,1,0:T(8,128)S(1)} %get-tuple-element.10, f32[128,128]{1,0:T(8,128)S(1)} %get-tuple-element.45, f32[128,128]{1,0:T(8,128)S(1)} %get-tuple-element.44, f32[128,128]{1,0:T(8,128)S(1)} %fusion.63), kind=kOutput, calls=%fused_computation.12 | convolution fusion | flops 4833607680 | bytes 12779520 | tf_op jit(solution)/shard_map/...kn,nm->...km/dot_general | solution.py:89
  155.8 5.3 %fusion.16 = f32[3,2,32,32,256]{4,3,2,1,0:T(8,128)S(1)} fusion(f32[3,2,32,32,128]{4,3,2,1,0:T(8,128)S(1)} %get-tuple-element.17, f32[3,2,32,32,128]{4,3,2,1,0:T(8,128)S(1)} %get-tuple-element.16, f32[128,128]{1,0:T(8,128)S(1)} %get-tuple-element.45, f32[128,128]{1,0:T(8,128)S(1)} %fusion.63, f32[128,128]{1,0:T(8,128)S(1)} %get-tuple-element.44), kind=kOutput, calls=%fused_computation.16 | convolution fusion | flops 4833607680 | bytes 12779520 | tf_op jit(solution)/shard_map/...kn,nm->...km/dot_general | solution.py:89
  162.1 5.3 %multiply_bitcast_fusion = f32[3,2,32,32,128]{4,3,2,1,0:T(8,128)} fusion(f32[3,2,32,32,128]{4,3,2,1,0:T(8,128)S(1)} %get-tuple-element.9, f32[3,2,32,32,128]{4,3,2,1,0:T(8,128)S(1)} %get-tuple-element.8, f32[32,32]{0,1:T(8,128)S(1)} %get-tuple-element.40, f32[32,32]{0,1:T(8,128)S(1)} %get-tuple-element.41), kind=kOutput, calls=%fused_computation.33 | convolution fusion | flops 606341120 | bytes 9445376 | tf_op jit(solution)/shard_map/kn,...nm->...km/dot_general | solution.py:85
  175.2 10.4 %all-to-all-done.1 = f32[16,3,4,16,256]{4,3,2,1,0:T(8,128)} async-done(((f32[16,3,4,16,256]{4,3,2,1,0:T(8,128)}), f32[16,3,4,16,256]{4,3,2,1,0:T(8,128)}, u32[]{:S(2)}, u32[]{:S(2)}) %all-to-all-start.1) | async-done | bytes 3145760 | tf_op jit(solution)/shard_map/all_to_all | solution.py:146
  188.0 7.3 %all_to_all.53 = f32[3,4,256,256]{3,2,0,1:T(8,128)} all-to-all(f32[3,4,256,256]{3,2,0,1:T(8,128)S(1)} %copy.124), channel_id=1, replica_groups=mesh['plane'=2,'row'=8,'col_0'=4,'col_1'=4] {'plane'}, dimensions={1} | all-to-all | bytes 6291456 | tf_op jit(solution)/shard_map/all_to_all | solution.py:148
  200.5 38.8 %all-to-all-done.4 = f32[8,3,2,256,32]{3,4,2,1,0:T(8,128)S(1)} async-done(((f32[8,3,2,256,32]{3,4,2,1,0:T(8,128)}), f32[8,3,2,256,32]{3,4,2,1,0:T(8,128)S(1)}, u32[]{:S(2)}, u32[]{:S(2)}) %all-to-all-start.4) | async-done | bytes 1572896 | tf_op jit(solution)/shard_map/all_to_all | solution.py:44
  239.3 4.3 %all-to-all-start.5 = ((f32[8,3,2,256,32]{3,4,2,1,0:T(8,128)}), f32[8,3,2,256,32]{3,4,2,1,0:T(8,128)}, u32[]{:S(2)}, u32[]{:S(2)}) async-start(f32[8,3,2,256,32]{3,4,2,1,0:T(8,128)} %copy.132), calls=%async_computation.5 | async-start | bytes 3145728 | tf_op jit(solution)/shard_map/all_to_all | solution.py:44
  245.9 35.9 %all-to-all-done.5 = f32[8,3,2,256,32]{3,4,2,1,0:T(8,128)} async-done(((f32[8,3,2,256,32]{3,4,2,1,0:T(8,128)}), f32[8,3,2,256,32]{3,4,2,1,0:T(8,128)}, u32[]{:S(2)}, u32[]{:S(2)}) %all-to-all-start.5) | async-done | bytes 1572896 | tf_op jit(solution)/shard_map/all_to_all | solution.py:44
  316.5 14.7 %psum.21 = f32[4,4]{1,0:T(4,128)S(1)} all-reduce(f32[4,4]{1,0:T(4,128)S(1)} %multiply_multiply_fusion.1), channel_id=1, replica_groups=mesh['plane'=2,'row'=8,'col_0'=4,'col_1'=4] {'row'}, use_global_device_ids=true, to_apply=%region_4.5 | all-reduce | flops 16 | bytes 128 | tf_op jit(solution)/shard_map/psum | solution.py:64
  331.2 9.7 %psum.22 = f32[4,4]{1,0:T(4,128)S(1)} all-reduce(f32[4,4]{1,0:T(4,128)S(1)} %psum.21), channel_id=1, replica_groups=mesh['plane'=2,'row'=8,'col_0'=4,'col_1'=4] {'col_0'}, use_global_device_ids=true, to_apply=%region_5.6 | all-reduce | flops 16 | bytes 128 | tf_op jit(solution)/shard_map/psum | solution.py:64
  341.0 12.0 %psum.23 = f32[4,4]{1,0:T(4,128)S(1)} all-reduce(f32[4,4]{1,0:T(4,128)S(1)} %psum.22), channel_id=1, replica_groups=mesh['plane'=2,'row'=8,'col_0'=4,'col_1'=4] {'col_1'}, use_global_device_ids=true, to_apply=%region_6.7 | all-reduce | flops 16 | bytes 128 | tf_op jit(solution)/shard_map/psum | solution.py:64
  354.1 3.9 %multiply_add_fusion.4 = f32[2,512,256]{2,1,0:T(8,128)} fusion(f32[2,512,256]{2,1,0:T(8,128)} %bitcast.189, f32[2,512,256]{2,1,0:T(8,128)} %copy.139, f32[2,512,256]{2,1,0:T(8,128)} %bitcast.188, f32[2,512,256]{2,1,0:T(8,128)} %copy.137, f32[2,512,256]{2,1,0:T(8,128)S(1)} %bitcast.187, f32[2,512,256]{2,1,0:T(8,128)} %copy.135), kind=kLoop, calls=%fused_computation.53 | loop fusion | flops 2097152 | bytes 7340032 | tf_op jit(solution)/shard_map/add | solution.py:152
  (99 shorter events, 101.4 us)
Async XLA Ops:
  4.7 7.9 %copy-start = (f32[3,2,512,256]{3,2,1,0:T(8,128)S(1)}, f32[3,2,512,256]{3,2,1,0:T(8,128)}, u32[]{:S(2)}) copy-start(f32[3,2,512,256]{3,2,1,0:T(8,128)} %param.1) | copy-start | bytes 9437188
  4.7 46.9 %all-to-all-start = ((f32[32,3,2,16,256]{4,3,2,1,0:T(8,128)}), f32[32,3,2,16,256]{4,3,2,1,0:T(8,128)}, u32[]{:S(2)}, u32[]{:S(2)}) async-start(f32[32,3,2,16,256]{4,3,2,1,0:T(8,128)} %bitcast.177), calls=%async_computation | async-start | bytes 6291456 | tf_op jit(solution)/shard_map/all_to_all | solution.py:54
  51.6 82.4 %all-to-all-start.3 = ((f32[3,2,512,256]{2,1,0,3:T(2,128)}), f32[3,2,512,256]{2,1,0,3:T(2,128)S(1)}, u32[]{:S(2)}, u32[]{:S(2)}) async-start(f32[3,2,512,256]{2,1,0,3:T(2,128)} %copy.127), calls=%async_computation.3 | async-start | bytes 6291456 | tf_op jit(solution)/shard_map/all_to_all | solution.py:138
  97.0 3.8 %copy-start.4 = (f32[3,3,16,4096]{3,2,1,0:T(8,128)S(1)}, f32[3,3,16,4096]{3,2,1,0:T(8,128)}, u32[]{:S(2)}) copy-start(f32[3,3,16,4096]{3,2,1,0:T(8,128)} %get-tuple-element.36) | copy-start | bytes 7077892
  97.0 3.8 %copy-start.5 = (f32[3,3,16,4096]{3,2,1,0:T(8,128)S(1)}, f32[3,3,16,4096]{3,2,1,0:T(8,128)}, u32[]{:S(2)}) copy-start(f32[3,3,16,4096]{3,2,1,0:T(8,128)} %get-tuple-element.37) | copy-start | bytes 7077892
  97.0 3.8 %copy-start.9 = (f32[3,1,16,4096]{3,2,1,0:T(8,128)S(1)}, f32[3,1,16,4096]{3,2,1,0:T(8,128)}, u32[]{:S(2)}) copy-start(f32[3,1,16,4096]{3,2,1,0:T(8,128)} %get-tuple-element.34) | copy-start | bytes 2359300
  97.0 3.8 %copy-start.10 = (f32[3,1,16,4096]{3,2,1,0:T(8,128)S(1)}, f32[3,1,16,4096]{3,2,1,0:T(8,128)}, u32[]{:S(2)}) copy-start(f32[3,1,16,4096]{3,2,1,0:T(8,128)} %get-tuple-element.35) | copy-start | bytes 2359300
  111.9 2.9 copy-start.8
  134.1 51.5 %all-to-all-start.1 = ((f32[16,3,4,16,256]{4,3,2,1,0:T(8,128)}), f32[16,3,4,16,256]{4,3,2,1,0:T(8,128)}, u32[]{:S(2)}, u32[]{:S(2)}) async-start(f32[16,3,4,16,256]{4,3,2,1,0:T(8,128)} %fusion.39), calls=%async_computation.1 | async-start | bytes 6291456 | tf_op jit(solution)/shard_map/all_to_all | solution.py:146
  195.2 44.0 %all-to-all-start.4 = ((f32[8,3,2,256,32]{3,4,2,1,0:T(8,128)}), f32[8,3,2,256,32]{3,4,2,1,0:T(8,128)S(1)}, u32[]{:S(2)}, u32[]{:S(2)}) async-start(f32[8,3,2,256,32]{3,4,2,1,0:T(8,128)} %copy.131), calls=%async_computation.4 | async-start | bytes 3145728 | tf_op jit(solution)/shard_map/all_to_all | solution.py:44
  239.3 4.3 %copy-start.6 = (f32[8,3,2,256,32]{3,4,2,1,0:T(8,128)}, f32[8,3,2,256,32]{3,4,2,1,0:T(8,128)S(1)}, u32[]{:S(2)}) copy-start(f32[8,3,2,256,32]{3,4,2,1,0:T(8,128)S(1)} %all-to-all-done.4) | copy-start | bytes 4718596
  239.3 42.6 %all-to-all-start.5 = ((f32[8,3,2,256,32]{3,4,2,1,0:T(8,128)}), f32[8,3,2,256,32]{3,4,2,1,0:T(8,128)}, u32[]{:S(2)}, u32[]{:S(2)}) async-start(f32[8,3,2,256,32]{3,4,2,1,0:T(8,128)} %copy.132), calls=%async_computation.5 | async-start | bytes 3145728 | tf_op jit(solution)/shard_map/all_to_all | solution.py:44
  304.4 3.1 copy-start.3
  305.4 3.5 copy-start.2
  306.5 3.7 %copy-start.1 = (f32[1,2,512,8,32]{2,4,3,1,0:T(8,128)S(1)}, f32[1,2,512,8,32]{2,4,3,1,0:T(8,128)}, u32[]{:S(2)}) copy-start(f32[1,2,512,8,32]{2,4,3,1,0:T(8,128)} %get-tuple-element.25) | copy-start | bytes 3145732
  310.2 43.9 %copy-start.7 = (f32[1,2,2,256,256]{4,3,2,1,0:T(8,128)S(1)}, f32[1,2,2,256,256]{4,3,2,1,0:T(8,128)}, u32[]{:S(2)}) copy-start(f32[1,2,2,256,256]{4,3,2,1,0:T(8,128)} %copy.126) | copy-start | bytes 3145732
